TPU v7x, 128 devices: a whole 4x4x4 slice. The times are simulated.
128 devices in a mesh: req: 32 (over z, y, core), head: 4 (over x).
Axes of the slice: x: 4, y: 4, z: 4, core: 2. Of those that a mesh axis runs over, the one named last changes fastest.
Arguments:
- hidden_in: bfloat16 [512, 2048], P(None, 'req'), may hold values from -6 to 6
- lengths: int32 [512], P('req'), may hold values from 16 to 3072, as said below
- w_qkv: bfloat16 [3, 2048, 2048], P(None, 'req', 'head'), may hold values from -4 to 4, as said below
- qk_gain: float32 [2, 2048], P(None, 'head'), may hold values from 0.25 to 1.75
- cache_keys: bfloat16 [131072, 2048], P('req', 'head'), may hold values from -240 to 240
- cache_values: bfloat16 [131072, 2048], P('req', 'head'), may hold values from -6 to 6
- w_out: bfloat16 [2048, 2048], P('req', 'head'), may hold values from -3 to 3, as said below
- norm_gain: float32 [2, 2048], P(None, 'req'), may hold values from 0.25 to 1.75
- w_gate_up: bfloat16 [2, 2048, 8192], P(None, 'req', 'head'), may hold values from -0.125 to 0.125
- w_down: bfloat16 [2048, 8192], P('req', 'head'), may hold values from -3 to 3, as said below
Outputs:
- hidden_out: bfloat16 [512, 2048], P(None, 'req')
- new_keys: bfloat16 [512, 2048], P('req', 'head')
- new_values: bfloat16 [512, 2048], P('req', 'head')
Inputs may be any that keep to these rules, and one draw needn't show every extreme that they name: `lengths`: in each aligned group of requests 8 * 16 * k to 8 * 16 * k + 8 * 16 - 1 exactly one request, at a place drawn from the seed, has length 3072; every other length lies between 16 and 64. `w_qkv`: entries have magnitude at most 26 / sqrt(2048). `w_out`: entries have magnitude at most 23 / sqrt(2048). `w_down`: entries have magnitude at most 23 / sqrt(8192).
All inputs are finite; a program needn't handle non-finite values.
Results may differ from a plain program's by a relative error of at most 0.015.
Values may be sent and summed in bfloat16 or wider, within the bound.
No kernel may reach another device: no remote copies, remote signals or barrier semaphores. Data moves between devices by JAX's collectives and lax.ppermute only.
A program may use at most 128 MiB of HBM per device.

v0:
```python
import jax
import jax.numpy as jnp
from jax import lax
from jax.sharding import PartitionSpec as P

HEAD_DIM = 128
EPS = 1e-06
THETA = 500000.0


def rotate(values, positions):
    half = values.shape[-1] // 2
    freqs = jnp.power(THETA, -(jnp.arange(half, dtype=jnp.float32) * 2.0 / values.shape[-1]))
    angles = positions.astype(jnp.float32)[:, None] * freqs[None, :]
    cosine = jnp.cos(angles)[:, None, :]
    sine = jnp.sin(angles)[:, None, :]
    first = values[..., :half]
    second = values[..., half:]
    return jnp.concatenate(
        [first * cosine - second * sine, second * cosine + first * sine], axis=-1
    )


def contract_last(left, right):
    return lax.dot_general(
        left, right, (((1,), (1,)), ((), ())), preferred_element_type=jnp.float32
    )


def body(
    hidden_in,
    lengths,
    w_qkv,
    qk_gain,
    cache_keys,
    cache_values,
    w_out,
    norm_gain,
    w_gate_up,
    w_down,
):
    rows_here = lengths.shape[0]
    width_here = w_qkv.shape[2]
    heads_here = width_here // HEAD_DIM
    units_here = w_gate_up.shape[2]
    full_width = width_here * lax.axis_size("head")
    model_width = hidden_in.shape[1] * lax.axis_size("req")
    selected = hidden_in
    product = jnp.einsum("bd,gdf->bgf", selected, w_qkv, preferred_element_type=jnp.float32)
    projected = lax.psum_scatter(
        product.reshape(rows_here * lax.axis_size("req"), 3 * width_here),
        "req",
        scatter_dimension=0,
        tiled=True,
    )
    query = projected[:, :width_here]
    key_new = projected[:, width_here : 2 * width_here]
    value_new = projected[:, 2 * width_here :].astype(jnp.bfloat16)
    query_squares, key_squares = lax.psum(
        (jnp.sum(query * query, axis=1), jnp.sum(key_new * key_new, axis=1)), "head"
    )
    query = query * lax.rsqrt(query_squares[:, None] / full_width + EPS) * qk_gain[0]
    key_new = key_new * lax.rsqrt(key_squares[:, None] / full_width + EPS) * qk_gain[1]
    query_rot = rotate(query.reshape(rows_here, heads_here, HEAD_DIM), lengths).astype(jnp.bfloat16)
    key_rot = rotate(key_new.reshape(rows_here, heads_here, HEAD_DIM), lengths).astype(jnp.bfloat16)
    value_heads = value_new.reshape(rows_here, heads_here, HEAD_DIM)
    scale = HEAD_DIM ** (-0.5)
    starts = jnp.cumsum(lengths) - lengths
    ends = starts + lengths
    own_score = jnp.sum(query_rot.astype(jnp.float32) * key_rot.astype(jnp.float32), axis=2) * scale
    pool_rows = cache_keys.shape[0]
    block = 512

    def attend_block(index, carry):
        running_max, running_total, running_sum = carry
        offset = index * block
        block_keys = lax.dynamic_slice_in_dim(cache_keys, offset, block, 0).reshape(
            block, heads_here, HEAD_DIM
        )
        block_values = lax.dynamic_slice_in_dim(cache_values, offset, block, 0).reshape(
            block, heads_here, HEAD_DIM
        )
        scores = (
            jnp.einsum("rhd,phd->rhp", query_rot, block_keys, preferred_element_type=jnp.float32)
            * scale
        )
        positions = offset + jnp.arange(block, dtype=jnp.int32)
        inside = (positions[None, :] >= starts[:, None]) & (positions[None, :] < ends[:, None])
        scores = jnp.where(inside[:, None, :], scores, -jnp.inf)
        new_max = jnp.maximum(running_max, jnp.max(scores, axis=2))
        weights = jnp.exp(scores - new_max[:, :, None]).astype(jnp.bfloat16)
        factor = jnp.exp(running_max - new_max)
        running_total = running_total * factor + jnp.sum(weights.astype(jnp.float32), axis=2)
        running_sum = running_sum * factor[:, :, None] + jnp.einsum(
            "rhp,phd->rhd", weights, block_values, preferred_element_type=jnp.float32
        )
        return (new_max, running_total, running_sum)

    steps_count = pool_rows // block
    initial = (own_score, jnp.ones_like(own_score), value_heads.astype(jnp.float32))
    final_max, final_total, final_sum = lax.fori_loop(0, steps_count, attend_block, initial)
    attended = (
        (final_sum / final_total[:, :, None]).astype(jnp.bfloat16).reshape(rows_here, width_here)
    )
    attn_part = contract_last(lax.all_gather(attended, "req", axis=0, tiled=True), w_out)
    attn_full = lax.psum(attn_part, "head")
    attn_power = lax.psum(jnp.sum(attn_full * attn_full, axis=1), "req")
    attn_normed = attn_full * lax.rsqrt(attn_power[:, None] / model_width + EPS) * norm_gain[0]
    hidden_mid = (hidden_in.astype(jnp.float32) + attn_normed).astype(jnp.bfloat16)
    selected = hidden_mid
    product = jnp.einsum("bd,gdf->bgf", selected, w_gate_up, preferred_element_type=jnp.float32)
    combined = lax.psum_scatter(
        product.reshape(rows_here * lax.axis_size("req"), 2 * units_here),
        "req",
        scatter_dimension=0,
        tiled=True,
    )
    gated = combined[:, :units_here]
    lifted = combined[:, units_here:]
    activated = (jax.nn.silu(gated) * lifted).astype(jnp.bfloat16)
    down_part = contract_last(lax.all_gather(activated, "req", axis=0, tiled=True), w_down)
    ffn_full = lax.psum(down_part, "head")
    ffn_power = lax.psum(jnp.sum(ffn_full * ffn_full, axis=1), "req")
    ffn_normed = ffn_full * lax.rsqrt(ffn_power[:, None] / model_width + EPS) * norm_gain[1]
    hidden_out = (hidden_mid.astype(jnp.float32) + ffn_normed).astype(jnp.bfloat16)
    return (hidden_out, key_rot.reshape(rows_here, width_here), value_new)


def solution(mesh):
    return jax.shard_map(
        body,
        mesh=mesh,
        in_specs=(
            P(None, "req"),
            P("req"),
            P(None, "req", "head"),
            P(None, "head"),
            P("req", "head"),
            P("req", "head"),
            P("req", "head"),
            P(None, "req"),
            P(None, "req", "head"),
            P("req", "head"),
        ),
        out_specs=(P(None, "req"), P("req", "head"), P("req", "head")),
        check_vma=False,
    )
```

profile of v0, /device:TPU:0, one launch (start us, length us, event | category | flops | bytes accessed | tf_op | source)
XLA Modules:
  0.0 528.0 jit_solution(12049688516893260932)
XLA Ops:
  7.2 3.3 fusion.7
  10.6 3.6 copy.52
  14.6 82.7 %reduce-scatter.5.cloned.1.call-done = f32[16,1536]{1,0:T(8,128)} async-done(((f32[512,1536]{1,0:T(8,128)}), f32[16,1536]{1,0:T(8,128)}) %reduce-scatter.5.cloned.1.call-update) | async-done | bytes 98320 | tf_op jit(solution)/shard_map/reduce_scatter | solution.py:50
  98.2 10.5 %all-reduce = (f32[16]{0:T(128)S(1)}, f32[16]{0:T(128)S(1)}) all-reduce(f32[16]{0:T(128)S(1)} %get-tuple-element.227, f32[16]{0:T(128)S(1)} %get-tuple-element.226), channel_id=1, replica_groups=mesh['req'=32,'head'=4] {'head'}, use_global_device_ids=true, to_apply=%region_4.0 | all-reduce | flops 32 | bytes 256 | tf_op jit(solution)/shard_map/psum | solution.py:59
  109.5 1.4 convert_bitcast_fusion
  111.3 20.6 %while.18 = (s32[]{:T(128)}, f32[16,4]{0,1:T(4,128)S(1)}, f32[16,4]{0,1:T(4,128)S(1)}, f32[16,4,128]{2,0,1:T(8,128)S(1)}, s32[16]{0:T(128)S(1)}, /*index=5*/s32[...) while((s32[]{:T(128)}, f32[16,4]{0,1:T(4,128)S(1)}, ...), condition=%wide.region_10.11_spmd.clone, body=%wide.region_7.10_spmd.clone.sunk | while | flops 17113800 | bytes 5742917 | solution.py:101
  111.4 1.3 constant_dynamic-slice_fusion.3
  114.0 1.3 constant_dynamic-slice_fusion.3
  116.6 1.3 constant_dynamic-slice_fusion.3
  119.2 1.3 constant_dynamic-slice_fusion.3
  121.8 1.3 constant_dynamic-slice_fusion.3
  124.3 1.3 constant_dynamic-slice_fusion.3
  132.1 24.1 %all_gather.6 = bf16[512,512]{1,0:T(8,128)(2,1)S(1)} all-gather(bf16[16,512]{1,0:T(8,128)(2,1)S(1)} %copy_bitcast_fusion.2), channel_id=1, replica_groups=mesh['req'=32,'head'=4] {'req'}, dimensions={0}, use_global_device_ids=true | all-gather | bytes 540672 | tf_op jit(solution)/shard_map/all_gather | solution.py:105
  157.3 37.5 %all-reduce.4.cloned.1.call-done = f32[512,64]{0,1:T(8,128)} async-done(((f32[512,64]{0,1:T(8,128)}), f32[512,64]{0,1:T(8,128)}) %all-reduce.4.cloned.1.call-update) | async-done | bytes 131088 | tf_op jit(solution)/shard_map/psum | solution.py:106
  195.7 65.2 %psum.45 = f32[512]{0:T(512)S(1)} all-reduce(f32[512]{0:T(512)S(1)} %multiply_reduce_fusion.1), channel_id=1, replica_groups=mesh['req'=32,'head'=4] {'req'}, use_global_device_ids=true, to_apply=%region_13.14 | all-reduce | flops 512 | bytes 4096 | tf_op jit(solution)/shard_map/psum | solution.py:107
  261.9 4.5 fusion.5
  266.4 8.9 %copy.69 = f32[512,4096]{1,0:T(8,128)} copy(f32[512,4096]{0,1:T(8,128)} %bitcast.64) | data formatting | bytes 16777216
  275.4 88.6 %reduce-scatter.7.cloned.1.call-done = f32[16,4096]{1,0:T(8,128)} async-done(((f32[512,4096]{1,0:T(8,128)}), f32[16,4096]{1,0:T(8,128)}) %reduce-scatter.7.cloned.1.call-update) | async-done | bytes 262160 | tf_op jit(solution)/shard_map/reduce_scatter | solution.py:112
  364.0 1.6 fusion.4
  365.7 44.5 %all-gather.2.cloned.1.call-done = bf16[512,2048]{1,0:T(8,128)(2,1)} async-done(((bf16[16,2048]{1,0:T(8,128)(2,1)}), bf16[512,2048]{1,0:T(8,128)(2,1)}) %all-gather.2.cloned.1.call-update) | async-done | bytes 2097168 | tf_op jit(solution)/shard_map/all_gather | solution.py:121
  410.2 3.0 fusion.16
  413.9 39.9 %all-reduce.6.cloned.1.call-done = f32[512,64]{0,1:T(8,128)} async-done(((f32[512,64]{0,1:T(8,128)}), f32[512,64]{0,1:T(8,128)}) %all-reduce.6.cloned.1.call-update) | async-done | bytes 131088 | tf_op jit(solution)/shard_map/psum | solution.py:122
  454.7 65.2 %psum.47 = f32[512]{0:T(512)S(1)} all-reduce(f32[512]{0:T(512)S(1)} %multiply_reduce_fusion), channel_id=1, replica_groups=mesh['req'=32,'head'=4] {'req'}, use_global_device_ids=true, to_apply=%region_17.18 | all-reduce | flops 512 | bytes 4096 | tf_op jit(solution)/shard_map/psum | solution.py:123
  519.8 1.6 add_convert_fusion
  (135 shorter events, 20.0 us)
Async XLA Ops:
  7.2 254.7 %copy-start = (bf16[2,64,2048]{2,1,0:T(8,128)(2,1)S(1)}, bf16[2,64,2048]{2,1,0:T(8,128)(2,1)}, u32[]{:S(2)}) copy-start(bf16[2,64,2048]{2,1,0:T(8,128)(2,1)} %param.20) | copy-start | bytes 1572868
  7.2 90.1 %reduce-scatter.5.cloned.1.call-start = ((), (), s32[]{:S(2)}) async-start(), calls=%async_computation.2 | async-start | bytes 3244032 | tf_op jit(solution)/shard_map/reduce_scatter | solution.py:50
  10.6 3.7 copy-start.5
  10.6 3.9 copy-start.4
  14.2 180.6 %all-reduce.4.cloned.1.call-start = ((), (), s32[]{:S(2)}) async-start(), calls=%async_computation.3 | async-start | bytes 262144 | tf_op jit(solution)/shard_map/psum | solution.py:106
  111.3 44.9 %copy-start.3 = (bf16[64,512]{1,0:T(8,128)(2,1)S(1)}, bf16[64,512]{1,0:T(8,128)(2,1)}, u32[]{:S(2)}) copy-start(bf16[64,512]{1,0:T(8,128)(2,1)} %param.18) | copy-start | bytes 196612
  111.3 45.9 %copy-start.6 = (f32[2,64]{1,0:T(2,128)S(1)}, f32[2,64]{1,0:T(2,128)}, u32[]{:S(2)}) copy-start(f32[2,64]{1,0:T(2,128)} %param.19) | copy-start | bytes 1540
  111.3 149.6 %copy-start.2 = (bf16[512,64]{0,1:T(8,128)(2,1)S(1)}, bf16[512,64]{0,1:T(8,128)(2,1)}, u32[]{:S(2)}) copy-start(bf16[512,64]{0,1:T(8,128)(2,1)} %param.12) | copy-start | bytes 196612
  157.2 206.8 %reduce-scatter.7.cloned.1.call-start = ((), (), s32[]{:S(2)}) async-start(), calls=%async_computation.6 | async-start | bytes 8650752 | tf_op jit(solution)/shard_map/reduce_scatter | solution.py:112
  275.3 134.9 %copy-start.1 = (bf16[64,2048]{1,0:T(8,128)(2,1)S(1)}, bf16[64,2048]{1,0:T(8,128)(2,1)}, u32[]{:S(2)}) copy-start(bf16[64,2048]{1,0:T(8,128)(2,1)} %param.21) | copy-start | bytes 786436
  275.4 134.9 %all-gather.2.cloned.1.call-start = ((), (), s32[]{:S(2)}) async-start(), calls=%async_computation.4 | async-start | bytes 2162688 | tf_op jit(solution)/shard_map/all_gather | solution.py:121
  365.7 88.1 %all-reduce.6.cloned.1.call-start = ((), (), s32[]{:S(2)}) async-start(), calls=%async_computation.5 | async-start | bytes 262144 | tf_op jit(solution)/shard_map/psum | solution.py:122
Sparse Core Ops, SparseCore 0:
  14.3 82.9 reduce-scatter.4
  157.3 37.4 all-reduce.3
  275.5 88.4 reduce-scatter.6
  367.0 43.2 all-gather.1
  413.4 40.3 all-reduce.5
where the time goes:
time: 529 us; the launch traced here: 528 us
  waiting for transfers between devices  293 us (55%)
  blocking collectives  165 us (31%)
  local copies, waits for them, and re-layouts  27.1 us (5%)
  matrix products  16.1 us (3%)
  between operations  13.9 us (3%)
  other arithmetic  12.2 us (2%)
    reduce_scatter x1, waiting for transfers between devices, body(): lax.psum_scatter(product.reshape(rows_here * lax.axis_size('req'), 2 * un...  88.6 us
    reduce_scatter x1, waiting for transfers between devices, body(): lax.psum_scatter(product.reshape(rows_here * lax.axis_size('req'), 3 * wi...  82.7 us
    psum x1, blocking collectives, body(): attn_power = lax.psum(jnp.sum(attn_full * attn_full, axis=1), 'req')  65.2 us
    psum x1, blocking collectives, body(): ffn_power = lax.psum(jnp.sum(ffn_full * ffn_full, axis=1), 'req')  65.2 us
    all_gather x1, waiting for transfers between devices, body(): lax.all_gather(activated, 'req', axis=0, tiled=True)  44.5 us
    psum x1, waiting for transfers between devices, body(): ffn_full = lax.psum(down_part, 'head')  39.9 us
    psum x1, waiting for transfers between devices, body(): attn_full = lax.psum(attn_part, 'head')  37.5 us
    all_gather x1, blocking collectives, body(): lax.all_gather(attended, 'req', axis=0, tiled=True)  24.1 us
  transfers between devices with their start and end apart: 5, of which 5 were waited for; matrix products, arithmetic and copies ran while one was open for 0% of the time, Pallas kernels for 0%

commit v1 on v0

--- a/solution.py
+++ b/solution.py
@@ -6,6 +6,11 @@
 HEAD_DIM = 128
 EPS = 1e-06
 THETA = 500000.0
+
+
+def gather_from_all(array, axis, dim):
+    copies = jnp.concatenate([array] * lax.axis_size(axis), axis=dim)
+    return lax.all_to_all(copies, axis, dim, dim, tiled=True)
 
 
 def rotate(values, positions):
@@ -102,7 +107,7 @@
     attended = (
         (final_sum / final_total[:, :, None]).astype(jnp.bfloat16).reshape(rows_here, width_here)
     )
-    attn_part = contract_last(lax.all_gather(attended, "req", axis=0, tiled=True), w_out)
+    attn_part = contract_last(gather_from_all(attended, "req", 0), w_out)
     attn_full = lax.psum(attn_part, "head")
     attn_power = lax.psum(jnp.sum(attn_full * attn_full, axis=1), "req")
     attn_normed = attn_full * lax.rsqrt(attn_power[:, None] / model_width + EPS) * norm_gain[0]

time: 529 us -> 523 us (0.989)
  blocking collectives: 165 us -> 157 us
    all_gather x1 -> x0, blocking collectives: 24.1 us -> none  [body(): lax.all_gather(attended, 'req', axis=0, tiled=True)]
    all_to_all x0 -> x1, blocking collectives: none -> 16.7 us  [gather_from_all(): return lax.all_to_all(copies, axis, dim, dim, tiled=True)]
where the time goes in v1:
time: 523 us; the launch traced here: 522 us
  waiting for transfers between devices  292 us (56%)
  blocking collectives  157 us (30%)
  local copies, waits for them, and re-layouts  27.1 us (5%)
  matrix products  16.1 us (3%)
  other arithmetic  14.7 us (3%)
  between operations  14.1 us (3%)
    reduce_scatter x1, waiting for transfers between devices, body(): lax.psum_scatter(product.reshape(rows_here * lax.axis_size('req'), 2 * un...  88.6 us
    reduce_scatter x1, waiting for transfers between devices, body(): lax.psum_scatter(product.reshape(rows_here * lax.axis_size('req'), 3 * wi...  82.7 us
    psum x1, blocking collectives, body(): ffn_power = lax.psum(jnp.sum(ffn_full * ffn_full, axis=1), 'req')  65.2 us
    psum x1, blocking collectives, body(): attn_power = lax.psum(jnp.sum(attn_full * attn_full, axis=1), 'req')  65.2 us
    all_gather x1, waiting for transfers between devices, body(): lax.all_gather(activated, 'req', axis=0, tiled=True)  44.5 us
    psum x1, waiting for transfers between devices, body(): ffn_full = lax.psum(down_part, 'head')  39.9 us
    psum x1, waiting for transfers between devices, body(): attn_full = lax.psum(attn_part, 'head')  36.7 us
    all_to_all x1, blocking collectives, gather_from_all(): return lax.all_to_all(copies, axis, dim, dim, tiled=True)  16.7 us
  transfers between devices with their start and end apart: 5, of which 5 were waited for; matrix products, arithmetic and copies ran while one was open for 0% of the time, Pallas kernels for 0%

profile of v1, /device:TPU:0, one launch (start us, length us, event | category | flops | bytes accessed | tf_op | source)
XLA Modules:
  0.0 522.5 jit_solution(6187824510059765378)
XLA Ops:
  7.2 3.3 fusion.7
  10.6 3.6 copy.52
  14.6 82.7 %reduce-scatter.5.cloned.1.call-done = f32[16,1536]{1,0:T(8,128)} async-done(((f32[512,1536]{1,0:T(8,128)}), f32[16,1536]{1,0:T(8,128)}) %reduce-scatter.5.cloned.1.call-update) | async-done | bytes 98320 | tf_op jit(solution)/shard_map/reduce_scatter | solution.py:55
  98.2 10.5 %all-reduce = (f32[16]{0:T(128)S(1)}, f32[16]{0:T(128)S(1)}) all-reduce(f32[16]{0:T(128)S(1)} %get-tuple-element.227, f32[16]{0:T(128)S(1)} %get-tuple-element.226), channel_id=1, replica_groups=mesh['req'=32,'head'=4] {'head'}, use_global_device_ids=true, to_apply=%region_4.0 | all-reduce | flops 32 | bytes 256 | tf_op jit(solution)/shard_map/psum | solution.py:64
  109.5 1.4 convert_bitcast_fusion
  111.3 20.7 %while.18 = (s32[]{:T(128)}, f32[16,4]{0,1:T(4,128)S(1)}, f32[16,4]{0,1:T(4,128)S(1)}, f32[16,4,128]{2,0,1:T(8,128)S(1)}, s32[16]{0:T(128)S(1)}, /*index=5*/s32[...) while((s32[]{:T(128)}, f32[16,4]{0,1:T(4,128)S(1)}, ...), condition=%wide.region_10.11_spmd.clone, body=%wide.region_7.10_spmd.clone.sunk | while | flops 17113800 | bytes 5742917 | solution.py:106
  111.4 1.3 constant_dynamic-slice_fusion.3
  114.0 1.3 constant_dynamic-slice_fusion.3
  116.6 1.3 constant_dynamic-slice_fusion.3
  121.8 1.3 constant_dynamic-slice_fusion.3
  124.4 1.3 constant_dynamic-slice_fusion.3
  129.5 1.3 constant_dynamic-slice_fusion.3
  134.8 16.7 %all_to_all.12 = bf16[32,16,512]{2,1,0:T(8,128)(2,1)S(1)} all-to-all(bf16[32,16,512]{2,1,0:T(8,128)(2,1)S(1)} %bitcast.132), channel_id=1, replica_groups=mesh['req'=32,'head'=4] {'req'}, dimensions={0} | all-to-all | bytes 1048576 | tf_op jit(solution)/shard_map/all_to_all | solution.py:13
  152.6 36.7 %all-reduce.4.cloned.1.call-done = f32[512,64]{0,1:T(8,128)} async-done(((f32[512,64]{0,1:T(8,128)}), f32[512,64]{0,1:T(8,128)}) %all-reduce.4.cloned.1.call-update) | async-done | bytes 131088 | tf_op jit(solution)/shard_map/psum | solution.py:111
  190.2 65.2 %psum.45 = f32[512]{0:T(512)S(1)} all-reduce(f32[512]{0:T(512)S(1)} %multiply_reduce_fusion.1), channel_id=1, replica_groups=mesh['req'=32,'head'=4] {'req'}, use_global_device_ids=true, to_apply=%region_13.14 | all-reduce | flops 512 | bytes 4096 | tf_op jit(solution)/shard_map/psum | solution.py:112
  256.3 4.5 fusion.5
  260.9 8.9 %copy.69 = f32[512,4096]{1,0:T(8,128)} copy(f32[512,4096]{0,1:T(8,128)} %bitcast.129) | data formatting | bytes 16777216
  269.9 88.6 %reduce-scatter.7.cloned.1.call-done = f32[16,4096]{1,0:T(8,128)} async-done(((f32[512,4096]{1,0:T(8,128)}), f32[16,4096]{1,0:T(8,128)}) %reduce-scatter.7.cloned.1.call-update) | async-done | bytes 262160 | tf_op jit(solution)/shard_map/reduce_scatter | solution.py:117
  358.5 1.6 fusion.4
  360.2 44.5 %all-gather.2.cloned.1.call-done = bf16[512,2048]{1,0:T(8,128)(2,1)} async-done(((bf16[16,2048]{1,0:T(8,128)(2,1)}), bf16[512,2048]{1,0:T(8,128)(2,1)}) %all-gather.2.cloned.1.call-update) | async-done | bytes 2097168 | tf_op jit(solution)/shard_map/all_gather | solution.py:126
  404.7 3.0 fusion.16
  408.4 39.9 %all-reduce.6.cloned.1.call-done = f32[512,64]{0,1:T(8,128)} async-done(((f32[512,64]{0,1:T(8,128)}), f32[512,64]{0,1:T(8,128)}) %all-reduce.6.cloned.1.call-update) | async-done | bytes 131088 | tf_op jit(solution)/shard_map/psum | solution.py:127
  449.2 65.2 %psum.47 = f32[512]{0:T(512)S(1)} all-reduce(f32[512]{0:T(512)S(1)} %multiply_reduce_fusion), channel_id=1, replica_groups=mesh['req'=32,'head'=4] {'req'}, use_global_device_ids=true, to_apply=%region_17.18 | all-reduce | flops 512 | bytes 4096 | tf_op jit(solution)/shard_map/psum | solution.py:128
  514.3 1.6 add_convert_fusion
  (166 shorter events, 22.5 us)
Async XLA Ops:
  7.2 249.2 %copy-start = (bf16[2,64,2048]{2,1,0:T(8,128)(2,1)S(1)}, bf16[2,64,2048]{2,1,0:T(8,128)(2,1)}, u32[]{:S(2)}) copy-start(bf16[2,64,2048]{2,1,0:T(8,128)(2,1)} %param.20) | copy-start | bytes 1572868
  7.2 90.1 %reduce-scatter.5.cloned.1.call-start = ((), (), s32[]{:S(2)}) async-start(), calls=%async_computation.3 | async-start | bytes 3244032 | tf_op jit(solution)/shard_map/reduce_scatter | solution.py:55
  10.6 3.7 copy-start.5
  10.6 3.9 copy-start.4
  14.2 175.1 %all-reduce.4.cloned.1.call-start = ((), (), s32[]{:S(2)}) async-start(), calls=%async_computation.4 | async-start | bytes 262144 | tf_op jit(solution)/shard_map/psum | solution.py:111
  111.3 40.2 %copy-start.3 = (bf16[64,512]{1,0:T(8,128)(2,1)S(1)}, bf16[64,512]{1,0:T(8,128)(2,1)}, u32[]{:S(2)}) copy-start(bf16[64,512]{1,0:T(8,128)(2,1)} %param.18) | copy-start | bytes 196612
  111.3 41.2 %copy-start.6 = (f32[2,64]{1,0:T(2,128)S(1)}, f32[2,64]{1,0:T(2,128)}, u32[]{:S(2)}) copy-start(f32[2,64]{1,0:T(2,128)} %param.19) | copy-start | bytes 1540
  111.3 144.0 %copy-start.2 = (bf16[512,64]{0,1:T(8,128)(2,1)S(1)}, bf16[512,64]{0,1:T(8,128)(2,1)}, u32[]{:S(2)}) copy-start(bf16[512,64]{0,1:T(8,128)(2,1)} %param.12) | copy-start | bytes 196612
  152.5 206.0 %reduce-scatter.7.cloned.1.call-start = ((), (), s32[]{:S(2)}) async-start(), calls=%async_computation.7 | async-start | bytes 8650752 | tf_op jit(solution)/shard_map/reduce_scatter | solution.py:117
  269.8 134.9 %copy-start.1 = (bf16[64,2048]{1,0:T(8,128)(2,1)S(1)}, bf16[64,2048]{1,0:T(8,128)(2,1)}, u32[]{:S(2)}) copy-start(bf16[64,2048]{1,0:T(8,128)(2,1)} %param.21) | copy-start | bytes 786436
  269.8 134.9 %all-gather.2.cloned.1.call-start = ((), (), s32[]{:S(2)}) async-start(), calls=%async_computation.5 | async-start | bytes 2162688 | tf_op jit(solution)/shard_map/all_gather | solution.py:126
  360.1 88.1 %all-reduce.6.cloned.1.call-start = ((), (), s32[]{:S(2)}) async-start(), calls=%async_computation.6 | async-start | bytes 262144 | tf_op jit(solution)/shard_map/psum | solution.py:127
Sparse Core Ops, SparseCore 0:
  14.3 82.9 reduce-scatter.4
  152.6 36.5 all-reduce.3
  269.9 88.4 reduce-scatter.6
  361.4 43.2 all-gather.1
  407.9 40.3 all-reduce.5
